TPU v7x, 32 devices: a whole 2x2x4 slice. The times are simulated.
32 devices in a mesh: dp: 2 (over y), seq: 16 (over z, x, core).
Axes of the slice: x: 2, y: 2, z: 4, core: 2. Of those that a mesh axis runs over, the one named last changes fastest.
Arguments:
- tokens: bfloat16 [2, 4096, 768], P('dp', 'seq'), may hold values from -9 to 9
- valid_mask: int32 [2, 4096], P('dp', 'seq'), may hold values from 0 to 1, as said below
- w_query: bfloat16 [768, 768], replicated, may hold values from -1 to 1
- w_key: bfloat16 [768, 768], replicated, may hold values from -1 to 1
- w_value: bfloat16 [768, 768], replicated, may hold values from -0.21875 to 0.21875
- w_out: bfloat16 [768, 768], replicated, may hold values from -0.21875 to 0.21875
- result_grad: bfloat16 [2, 4096, 768], P('dp', 'seq'), may hold values from -6 to 6
Outputs:
- result: bfloat16 [2, 4096, 768], P('dp', 'seq')
- token_grads: bfloat16 [2, 4096, 768], P('dp', 'seq')
- weight_grads: float32 [4, 768, 768], P(None, 'seq')
Inputs may be any that keep to these rules, and one draw needn't show every extreme that they name: `valid_mask`: in every sequence the positions whose index modulo 64 is below 8 are 1.
All inputs are finite; a program needn't handle non-finite values.
Results may differ from a plain program's by a relative error of at most 0.0095.
Values may be sent and summed in bfloat16 or wider, within the bound.
A program may use at most 128 MiB of HBM per device.

v0:
```python
import functools
import math

import jax
import jax.numpy as jnp
from jax import lax
from jax.experimental import pallas as pl
from jax.experimental.pallas import tpu as pltpu
from jax.sharding import PartitionSpec as P

HEADS = 16
HEAD_DIM = 48
GROUPS = 4
PER_GROUP = HEADS // GROUPS
LANES = 128
HALF = 64
WINDOW = 256
MASKED = -1e30
F32 = jnp.float32
BF16 = jnp.bfloat16
MESH = pl.DeviceIdType.MESH


def dot_nn(a, b):
    return lax.dot_general(a, b, (((1,), (0,)), ((), ())), preferred_element_type=F32)


def dot_nt(a, b):
    return lax.dot_general(a, b, (((1,), (1,)), ((), ())), preferred_element_type=F32)


def dot_tn(a, b):
    return lax.dot_general(a, b, (((0,), (0,)), ((), ())), preferred_element_type=F32)


class Plan:
    def __init__(self, seq, length):
        self.seq = seq
        self.length = length
        self.sizes = [seq * 2**g // 2 ** (GROUPS - 1) for g in range(GROUPS)]
        self.rows = [length // 2**g for g in range(GROUPS)]
        self.unit_rows = self.sizes[0] * length
        self.first_slot = []
        slots = 0
        for size in self.sizes:
            if size <= PER_GROUP:
                self.first_slot.append(slots)
                slots += PER_GROUP // size
            else:
                self.first_slot.append(None)
        self.extra = slots
        self.slots = slots + 1

    def start(self, group, head):
        quarter = self.length // 4
        if group == 0:
            return 0
        if group == 1:
            return head % 2 * (2 * quarter)
        return head % 2 * (2 * quarter) + head // 2 * quarter

    def place(self, group, head, base):
        size = self.sizes[group]
        if size <= PER_GROUP:
            each = PER_GROUP // size
            return base + head // each, self.first_slot[group] + head % each
        stride = size // PER_GROUP
        return base + head * stride + stride // 2 - 1, self.extra

    def groups_of_slot(self, slot):
        if slot == self.extra:
            return [(g, 0) for g in range(GROUPS) if self.sizes[g] > PER_GROUP]
        for g in reversed(range(GROUPS)):
            if self.first_slot[g] is not None and slot >= self.first_slot[g]:
                return [(g, slot - self.first_slot[g])]

    def owned(self, group, index, me):
        size = self.sizes[group]
        if size <= PER_GROUP:
            each = PER_GROUP // size
            return None, me % size * each + index
        stride = size // PER_GROUP
        return me % stride == stride // 2 - 1, me % size // stride


def guarded(condition, body):
    if condition is None:
        body()
    else:
        pl.when(condition)(body)


def spread_matrix(offset, high):
    row = lax.broadcasted_iota(jnp.int32, (WINDOW, PER_GROUP * LANES), 0)
    col = lax.broadcasted_iota(jnp.int32, (WINDOW, PER_GROUP * LANES), 1)
    lane = (col & (LANES - 1)) - (HALF if high else 0)
    head = col >> 7
    hit = (lane >= 0) & (lane < HEAD_DIM) & (row == offset + HEAD_DIM * head + lane)
    return hit.astype(F32).astype(BF16)


def window_of(group):
    first = group * PER_GROUP * HEAD_DIM
    begin = first // LANES * LANES
    return begin, first - begin


def permutation(length):
    eighth = length // 8
    bits = eighth.bit_length() - 1
    row = lax.broadcasted_iota(jnp.int32, (length, length), 0)
    col = lax.broadcasted_iota(jnp.int32, (length, length), 1)
    block = row >> bits
    residue = ((block & 1) << 2) | (block & 2) | (block >> 2)
    return col == ((row & (eighth - 1)) << 3) + residue


def attend(units, outs, slot, scale):
    tile0 = units[slot, 0]
    tile1 = units[slot, 1]
    low = lax.broadcasted_iota(jnp.int32, tile0.shape, 1) < HALF
    zero = jnp.zeros_like(tile0)
    scores = dot_nt(jnp.where(low, tile0, zero), tile1) * scale
    top = jnp.max(scores, axis=-1, keepdims=True)
    weights = jnp.exp(scores - top)
    probs = weights * (1.0 / jnp.sum(weights, axis=-1, keepdims=True))
    probs_bf = probs.astype(BF16)
    head_out = dot_nn(probs_bf, tile1)
    grad = jnp.where(low, zero, tile0)
    delta = jnp.sum(grad.astype(F32) * head_out, axis=-1, keepdims=True)
    score_grads = (scale * probs * (dot_nt(grad, tile1) - delta)).astype(BF16)
    outs[slot, 0] = jnp.where(low, dot_nn(score_grads, tile1), head_out).astype(BF16)
    outs[slot, 1] = jnp.where(low, dot_tn(score_grads, tile0), dot_tn(probs_bf, tile0)).astype(BF16)


def layer_kernel(plan, rows_each, *refs):
    (x_ref, mask_ref, wq_ref, wk_ref, wv_ref, wo_ref, g_ref) = refs[:7]
    result_ref, tgrad_ref, wgrad_ref = refs[7:10]
    staged = refs[10 : 10 + GROUPS]
    (units, outs, back, acc, send_sem, recv_sem, ret_send, ret_recv) = refs[10 + GROUPS :]
    length, seq = plan.length, plan.seq
    scale = 1.0 / math.sqrt(HEAD_DIM)
    me = lax.axis_index("seq")

    back[...] = jnp.zeros_like(back)
    barrier = pltpu.get_barrier_semaphore()
    for step in range(1, seq):
        pl.semaphore_signal(
            barrier, inc=1, device_id={"seq": lax.rem(me + step, seq)}, device_id_type=MESH
        )

    perm = permutation(length)
    perm_f = perm.astype(F32)
    perm_bf = perm_f.astype(BF16)
    x = dot_nn(perm_bf, x_ref[...]).astype(BF16)
    g = dot_nn(perm_bf, g_ref[...]).astype(BF16)
    bias_row = jnp.where(mask_ref[...] == 1, 0.0, MASKED)
    bias = jnp.sum(jnp.where(perm, jnp.broadcast_to(bias_row, perm.shape), 0.0), axis=1, keepdims=True)
    queries = dot_nn(x, wq_ref[...]).astype(BF16)
    keys = dot_nn(x, wk_ref[...]).astype(BF16)
    values = dot_nn(x, wv_ref[...]).astype(BF16)
    grads = dot_nt(g, wo_ref[...]).astype(BF16)
    lane = lax.broadcasted_iota(jnp.int32, (length, PER_GROUP * LANES), 1) & (LANES - 1)
    spreads = {}
    for group in range(GROUPS):
        begin, offset = window_of(group)
        if offset not in spreads:
            spreads[offset] = (spread_matrix(offset, False), spread_matrix(offset, True))
    for group in reversed(range(GROUPS)):
        begin, offset = window_of(group)
        low, high = spreads[offset]
        cut = slice(begin, begin + WINDOW)
        tile0 = dot_nn(queries[:, cut], low) + dot_nn(grads[:, cut], high)
        tile1 = dot_nn(keys[:, cut], low) + dot_nn(values[:, cut], high)
        tile0 = jnp.where(lane == HEAD_DIM, 1.0, tile0).astype(BF16)
        tile1 = jnp.where(lane == HEAD_DIM, bias, tile1).astype(BF16)
        for head in range(PER_GROUP):
            first = plan.start(group, head)
            rows = slice(first, first + plan.rows[group])
            lanes = slice(head * LANES, (head + 1) * LANES)
            staged[group][head, 0] = tile0[rows, lanes]
            staged[group][head, 1] = tile1[rows, lanes]

    pl.semaphore_wait(barrier, seq - 1)

    def out_copies(group):
        size = plan.sizes[group]
        base = me - me % size
        rows = plan.rows[group]
        row = pl.multiple_of(me % size * rows, rows)
        for head in range(PER_GROUP):
            owner, slot = plan.place(group, head, base)
            source = staged[group].at[head]
            target = units.at[slot, :, pl.ds(row, rows), :]
            remote = functools.partial(
                pltpu.make_async_remote_copy,
                source, target, send_sem.at[group, head], recv_sem.at[slot],
                device_id={"seq": owner}, device_id_type=MESH,
            )
            local = functools.partial(pltpu.make_async_copy, source, target, recv_sem.at[slot])
            yield owner, remote, local

    for group in reversed(range(GROUPS)):
        for owner, remote, local in out_copies(group):
            pl.when(owner != me)(lambda: remote().start())
            pl.when(owner == me)(lambda: local().start())

    def returns(slot, group, index, head):
        size = plan.sizes[group]
        base = me - me % size
        rows = plan.rows[group]
        first = pl.multiple_of(plan.start(group, head), plan.length // 8)
        for step in range(size):
            j = lax.rem(me + step, size)
            source = outs.at[slot, :, pl.ds(pl.multiple_of(j * rows, rows), rows), :]
            target = back.at[group, head, :, pl.ds(first, rows), :]
            if step == 0:
                yield None, pltpu.make_async_copy(source, target, ret_recv.at[group])
            else:
                yield step, pltpu.make_async_remote_copy(
                    source, target, ret_send.at[slot, step], ret_recv.at[group],
                    device_id={"seq": base + j}, device_id_type=MESH,
                )

    def start_all(slot, group, index, head):
        for _, copy in returns(slot, group, index, head):
            copy.start()

    def wait_sends(slot, group, index, head):
        for step, copy in returns(slot, group, index, head):
            if step is not None:
                copy.wait_send()

    order = list(range(plan.slots))
    for slot in order:
        entries = plan.groups_of_slot(slot)
        if not entries:
            continue
        owned = [(group, index) + plan.owned(group, index, me) for group, index in entries]
        conditions = [o[2] for o in owned if o[2] is not None]
        active = functools.reduce(jnp.logical_or, conditions) if conditions else None

        def work(slot=slot):
            pltpu.make_async_copy(units.at[slot], units.at[slot], recv_sem.at[slot]).wait()
            attend(units, outs, slot, scale)

        guarded(active, work)
        for group, index, condition, head in owned:
            guarded(condition, functools.partial(start_all, slot, group, index, head))

    for group in reversed(range(GROUPS)):
        for owner, remote, local in out_copies(group):
            pl.when(owner != me)(lambda: remote().wait_send())

    acc[...] = jnp.zeros_like(acc)
    for group in range(GROUPS):
        pltpu.make_async_copy(staged[group], staged[group], ret_recv.at[group]).wait()
        begin, offset = window_of(group)
        low, high = spreads[offset]
        for tile in range(2):
            packed = jnp.concatenate([back[group, head, tile] for head in range(PER_GROUP)], axis=1)
            acc[2 * tile, :, begin : begin + WINDOW] += dot_nt(packed, low)
            acc[2 * tile + 1, :, begin : begin + WINDOW] += dot_nt(packed, high)
    for slot in order:
        for group, index in plan.groups_of_slot(slot):
            condition, head = plan.owned(group, index, me)
            guarded(condition, functools.partial(wait_sends, slot, group, index, head))

    query_rows = acc[0].astype(BF16)
    attention = acc[1].astype(BF16)
    key_rows = acc[2].astype(BF16)
    value_rows = acc[3].astype(BF16)
    pairs = [(x, query_rows), (x, key_rows), (x, value_rows), (attention, g)]
    for which, (left, right) in enumerate(pairs):
        product = dot_tn(left, right).astype(wgrad_ref.dtype)
        for target in range(seq):
            wgrad_ref[target, which] = product[target * rows_each : (target + 1) * rows_each]
    result = dot_nn(attention, wo_ref[...]).astype(BF16)
    result_ref[...] = dot_tn(perm_bf, result).astype(BF16)
    token = (
        dot_nt(query_rows, wq_ref[...])
        + dot_nt(key_rows, wk_ref[...])
        + dot_nt(value_rows, wv_ref[...])
    ).astype(BF16)
    tgrad_ref[...] = dot_tn(perm_bf, token).astype(BF16)


def run_layer(seq, x, mask, wq, wk, wv, wo, g, wgrad_dtype):
    length, width = x.shape
    plan = Plan(seq, length)
    rows_each = width // seq
    vmem = pl.BlockSpec(memory_space=pltpu.VMEM)
    return pl.pallas_call(
        functools.partial(layer_kernel, plan, rows_each),
        out_shape=(
            jax.ShapeDtypeStruct((length, width), BF16),
            jax.ShapeDtypeStruct((length, width), BF16),
            jax.ShapeDtypeStruct((seq, 4, rows_each, width), wgrad_dtype),
        ),
        in_specs=[vmem] * 7,
        out_specs=[vmem] * 3,
        scratch_shapes=[
            pltpu.VMEM((PER_GROUP, 2, plan.rows[group], LANES), BF16) for group in range(GROUPS)
        ]
        + [
            pltpu.VMEM((plan.slots, 2, plan.unit_rows, LANES), BF16),
            pltpu.VMEM((plan.slots, 2, plan.unit_rows, LANES), BF16),
            pltpu.VMEM((GROUPS, PER_GROUP, 2, length, LANES), BF16),
            pltpu.VMEM((4, length, width), F32),
            pltpu.SemaphoreType.DMA((GROUPS, PER_GROUP)),
            pltpu.SemaphoreType.DMA((plan.slots,)),
            pltpu.SemaphoreType.DMA((plan.slots, seq)),
            pltpu.SemaphoreType.DMA((GROUPS,)),
        ],
        compiler_params=pltpu.CompilerParams(
            collective_id=0, has_side_effects=True, vmem_limit_bytes=60 * 2**20
        ),
        name="layer",
    )(x, mask, wq, wk, wv, wo, g)


BITS = 4
STREAMS = ((1, 2, 3), (2, 3, 1))


def reduce_kernel(parts, out_ref, data, *refs):
    recvs = refs[:-3]
    send_sem, recv_sem, load_sem = refs[-3:]
    me = lax.axis_index("seq")
    dp = lax.axis_index("dp")
    bit = [me // 2**k % 2 for k in range(BITS)]
    barrier = pltpu.get_barrier_semaphore()
    for k in range(BITS):
        pl.semaphore_signal(
            barrier, inc=1, device_id={"seq": me + 2**k - bit[k] * 2 ** (k + 1)}, device_id_type=MESH
        )
    pl.semaphore_signal(barrier, inc=1, device_id={"dp": 1 - dp}, device_id_type=MESH)
    load = pltpu.make_async_copy(parts, data, load_sem)
    load.start()
    load.wait()
    pl.semaphore_wait(barrier, BITS + 1)

    def view(fixed, m):
        index = [fixed.get(3 - d, slice(None)) for d in range(BITS)]
        return tuple(index) + (m,)

    def send(number, k, done, stream):
        fixed = {b: bit[b] for b in done}
        fixed[k] = 1 - bit[k]
        return pltpu.make_async_remote_copy(
            data.at[view(fixed, pl.ds(2 * stream, 2))], recvs[number], send_sem.at[number],
            recv_sem.at[number],
            device_id={"seq": me + 2**k - bit[k] * 2 ** (k + 1)}, device_id_type=MESH,
        )

    def add(number, k, done, stream):
        fixed = {b: bit[b] for b in done}
        fixed[k] = bit[k]
        mine = view(fixed, pl.ds(2 * stream, 2))
        data[mine] = (data[mine].astype(F32) + recvs[number][...].astype(F32)).astype(BF16)

    sequences = [(0,) + s for s in STREAMS]
    copies = []
    for stage in range(BITS):
        for stream in range(2):
            number = stage * 2 + stream
            if stage > 0:
                before = number - 2
                copies[before].wait_recv()
                add(before, sequences[stream][stage - 1], sequences[stream][: stage - 1], stream)
            copies.append(send(number, sequences[stream][stage], sequences[stream][:stage], stream))
            copies[-1].start()
    final = []
    for stream in range(2):
        before = (BITS - 1) * 2 + stream
        number = BITS * 2 + stream
        copies[before].wait_recv()
        add(before, sequences[stream][BITS - 1], sequences[stream][: BITS - 1], stream)
        mine = view(dict(enumerate(bit)), pl.ds(2 * stream, 2))
        final.append(
            pltpu.make_async_remote_copy(
                data.at[mine], recvs[number], send_sem.at[number], recv_sem.at[number],
                device_id={"dp": 1 - dp}, device_id_type=MESH,
            )
        )
        final[-1].start()
    for stream in range(2):
        mine = view(dict(enumerate(bit)), pl.ds(2 * stream, 2))
        final[stream].wait_recv()
        out_ref[2 * stream : 2 * stream + 2] = (
            data[mine].astype(F32) + recvs[BITS * 2 + stream][...].astype(F32)
        )
    for copy in copies + final:
        copy.wait_send()


def reduce_parts(parts, rows_each, width):
    parts = parts.reshape(2, 2, 2, 2, 4, rows_each, width)
    recvs = []
    for stage in range(BITS):
        recvs += [pltpu.VMEM((2,) * (BITS - 1 - stage) + (2, rows_each, width), BF16)] * 2
    recvs += [pltpu.VMEM((2, rows_each, width), BF16)] * 2
    return pl.pallas_call(
        reduce_kernel,
        out_shape=jax.ShapeDtypeStruct((4, rows_each, width), F32),
        in_specs=[pl.BlockSpec(memory_space=pl.ANY)],
        out_specs=pl.BlockSpec(memory_space=pltpu.VMEM),
        scratch_shapes=[pltpu.VMEM(parts.shape, BF16)]
        + recvs
        + [
            pltpu.SemaphoreType.DMA((2 * BITS + 2,)),
            pltpu.SemaphoreType.DMA((2 * BITS + 2,)),
            pltpu.SemaphoreType.DMA,
        ],
        compiler_params=pltpu.CompilerParams(
            collective_id=1, has_side_effects=True, vmem_limit_bytes=60 * 2**20
        ),
        name="reduce",
    )(parts)


def per_device(tokens, valid_mask, w_query, w_key, w_value, w_out, result_grad):
    seq, dp = lax.axis_size("seq"), lax.axis_size("dp")
    width = tokens.shape[2]
    rows_each = width // seq
    direct = seq == 2**BITS and dp == 2
    result, token_grads, parts = run_layer(
        seq, tokens[0], valid_mask, w_query, w_key, w_value, w_out, result_grad[0],
        BF16 if direct else F32,
    )
    if direct:
        weight_grads = reduce_parts(parts, rows_each, width)
    else:
        content = parts.reshape(seq, dp, -1).transpose(1, 0, 2).reshape(-1)
        share = lax.psum_scatter(content, ("dp", "seq"), scatter_dimension=0, tiled=True)
        weight_grads = lax.all_gather(share, "dp", axis=0, tiled=True).reshape(4, rows_each, width)
    return (result[None], token_grads[None], weight_grads)


def solution(mesh):
    return jax.shard_map(
        per_device,
        mesh=mesh,
        in_specs=(P("dp", "seq", None), P("dp", "seq"), P(), P(), P(), P(), P("dp", "seq", None)),
        out_specs=(P("dp", "seq", None), P("dp", "seq", None), P(None, "seq", None)),
        check_vma=False,
    )
```

profile of v0, /device:TPU:0, one launch (start us, length us, event | category | flops | bytes accessed | tf_op | source)
XLA Modules:
  0.0 86.3 jit_solution(7409858653407070465)
XLA Ops:
  0.6 29.5 %layer.1 = (bf16[256,768]{1,0:T(8,128)(2,1)}, bf16[256,768]{1,0:T(8,128)(2,1)}, bf16[16,4,48,768]{3,2,1,0:T(8,128)(2,1)}) custom-call(bf16[256,768]{1,0:T(8,128)(2,1)} %bitcast.6, s32[1,256]{1,0:T(1,128)} %refs_1_.1, bf16[768,768]{1,0:T(8,128)(2,1)} %refs_2_.1, bf16[768,768]{1,0:T(8,128)(2,1)} %refs_3_.1, bf16[768,768]{1,0:T(8,128)(2,1)} %refs_4_.1, ...), custom_call_target="tpu_custom_call" | custom-call | tf_op jit(solution)/shard_map/layer/pallas_call | solution.py:293
  30.1 0.0 copy-start.2
  30.1 0.0 copy-start.1
  30.2 53.8 %reduce.1 = f32[4,48,768]{2,1,0:T(8,128)} custom-call(bf16[2,2,2,2,4,48,768]{6,5,4,3,2,1,0:T(8,128)(2,1)} %bitcast.5), custom_call_target="tpu_custom_call" | custom-call | tf_op jit(solution)/shard_map/reduce/pallas_call | solution.py:403
  84.0 0.0 copy-done.2
  84.0 0.0 copy-start
  84.0 0.7 copy.13
  84.7 0.0 copy-done.1
  84.7 0.7 copy.14
  85.5 0.0 copy-done
  85.5 0.8 copy.15
Async XLA Ops:
  30.1 53.8 %copy-start.2 = (bf16[256,768]{1,0:T(8,128)(2,1)S(1)}, bf16[256,768]{1,0:T(8,128)(2,1)}, u32[]{:S(2)}) copy-start(bf16[256,768]{1,0:T(8,128)(2,1)} %get-tuple-element.6) | copy-start | bytes 1179652
  30.1 54.6 %copy-start.1 = (bf16[256,768]{1,0:T(8,128)(2,1)S(1)}, bf16[256,768]{1,0:T(8,128)(2,1)}, u32[]{:S(2)}) copy-start(bf16[256,768]{1,0:T(8,128)(2,1)} %get-tuple-element.7) | copy-start | bytes 1179652
  84.0 1.5 %copy-start = (f32[4,48,768]{2,1,0:T(8,128)S(1)}, f32[4,48,768]{2,1,0:T(8,128)}, u32[]{:S(2)}) copy-start(f32[4,48,768]{2,1,0:T(8,128)} %reduce.1) | copy-start | bytes 1769476
where the time goes:
time: 86.5 us; the launch traced here: 86.3 us
  Pallas kernels  83.3 us (96%)
  local copies, waits for them, and re-layouts  2.32 us (3%)
    pallas_call x1, Pallas kernels, reduce_parts(): pl.pallas_call(reduce_kernel, out_shape=jax.ShapeDtypeStruct((4, rows_eac...  53.8 us
    pallas_call x1, Pallas kernels, run_layer(): pl.pallas_call(functools.partial(layer_kernel, plan, rows_each), out_shap...  29.5 us
    unnamed x9, local copies, waits for them, and re-layouts  2.32 us

commit v1 on v0

--- a/solution.py
+++ b/solution.py
@@ -133,20 +133,149 @@
     outs[slot, 1] = jnp.where(low, dot_tn(score_grads, tile0), dot_tn(probs_bf, tile0)).astype(BF16)
 
 
-def layer_kernel(plan, rows_each, *refs):
-    (x_ref, mask_ref, wq_ref, wk_ref, wv_ref, wo_ref, g_ref) = refs[:7]
+BITS = 4
+CHUNK = 16
+Y = BITS
+FIRST_X, FIRST_Y, FIRST_Z = (1, Y, 2, 3), (Y, 1, 2, 3), (2, 3, 1, Y)
+
+
+def chunk_orders(rows_each):
+    pattern = (FIRST_Z, FIRST_X, FIRST_Y)
+    chunks = []
+    for which in range(4):
+        for index in range(rows_each // CHUNK):
+            order = pattern[index % 3]
+            if which == 3 and order is FIRST_Z:
+                order = FIRST_X
+            chunks.append((which, index * CHUNK, order))
+    return chunks
+
+
+def chunk_shapes(rows_each, width):
+    shapes = []
+    for _, _, order in chunk_orders(rows_each):
+        open_dims = {3, 2, 1, Y}
+        for axis in order:
+            open_dims.remove(axis)
+            shapes.append((2,) * len(open_dims) + (CHUNK, width // 2))
+    return shapes
+
+
+class Reducer:
+    def __init__(self, rows_each, data, core, final, recvs, core_sems, sems, final_sems):
+        self.data, self.core, self.final, self.recvs = data, core, final, recvs
+        self.core_sems, self.sems, self.final_sems = core_sems, sems, final_sems
+        self.chunks = chunk_orders(rows_each)
+        self.me = lax.axis_index("seq")
+        self.dp = lax.axis_index("dp")
+        self.bit = [self.me // 2**k % 2 for k in range(BITS)] + [self.dp]
+        self.started = []
+        self.current = {}
+
+    def peer(self, axis):
+        if axis == Y:
+            return {"dp": 1 - self.dp}
+        return {"seq": self.me + 2**axis - self.bit[axis] * 2 ** (axis + 1)}
+
+    def view(self, fixed, which, rows):
+        index = [fixed.get(3 - d, slice(None)) for d in range(BITS)]
+        return tuple(index) + (which, fixed.get(Y, slice(None)), rows)
+
+    def copy(self, source, target, sems, number, axis):
+        copy = pltpu.make_async_remote_copy(
+            source, target, sems.at[0, number], sems.at[1, number],
+            device_id=self.peer(axis), device_id_type=MESH,
+        )
+        copy.start()
+        self.started.append(copy)
+        return copy
+
+    def core_start(self, which):
+        other = self.view({0: 1 - self.bit[0]}, which, slice(None))
+        self.current["core", which] = self.copy(
+            self.data.at[other], self.core.at[which], self.core_sems, which, 0
+        )
+
+    def core_add(self, which):
+        self.current["core", which].wait_recv()
+        mine = self.view({0: self.bit[0]}, which, slice(None))
+        self.data[mine] = (
+            self.data[mine].astype(F32) + self.core[which].astype(F32)
+        ).astype(BF16)
+
+    def fixed(self, order, stage):
+        return {axis: self.bit[axis] for axis in (0,) + order[:stage]}
+
+    def start(self, number, stage):
+        which, row, order = self.chunks[number]
+        rows = pl.ds(row, CHUNK)
+        if stage == len(order):
+            mine = self.view(self.fixed(order, stage), which, rows)
+            self.current[number] = self.copy(
+                self.data.at[mine], self.final.at[which, rows], self.final_sems, number, Y
+            )
+            return
+        fixed = self.fixed(order, stage)
+        fixed[order[stage]] = 1 - self.bit[order[stage]]
+        slot = number * len(order) + stage
+        self.current[number] = self.copy(
+            self.data.at[self.view(fixed, which, rows)], self.recvs[slot], self.sems, slot,
+            order[stage],
+        )
+
+    def add(self, number, stage):
+        self.current[number].wait_recv()
+        which, row, order = self.chunks[number]
+        mine = self.view(self.fixed(order, stage + 1), which, pl.ds(row, CHUNK))
+        got = self.recvs[number * len(order) + stage][...]
+        self.data[mine] = (self.data[mine].astype(F32) + got.astype(F32)).astype(BF16)
+
+    def numbers(self, which):
+        return [n for n, chunk in enumerate(self.chunks) if chunk[0] == which]
+
+    def finish(self, out_ref):
+        numbers = sorted(range(len(self.chunks)), key=lambda n: self.chunks[n][2] is FIRST_Z)
+        for stage in range(4):
+            for number in numbers:
+                self.add(number, stage)
+                self.start(number, stage + 1)
+        for number in numbers:
+            self.current[number].wait_recv()
+        own_at = self.view(dict(enumerate(self.bit)), slice(None), slice(None))
+        own = self.data[own_at].astype(F32)
+        other = self.final[...].astype(F32)
+        half = out_ref.shape[2] // 2
+        low = self.dp == 0
+        out_ref[:, :, :half] = jnp.where(low, own, other)
+        out_ref[:, :, half:] = jnp.where(low, other, own)
+        for copy in self.started:
+            copy.wait_send()
+
+
+def layer_kernel(plan, rows_each, direct, *refs):
+    (x_ref, mask_ref, *weight_hbm, g_ref) = refs[:7]
     result_ref, tgrad_ref, wgrad_ref = refs[7:10]
     staged = refs[10 : 10 + GROUPS]
-    (units, outs, back, acc, send_sem, recv_sem, ret_send, ret_recv) = refs[10 + GROUPS :]
+    refs = refs[10 + GROUPS :]
+    (units, outs, back, acc, send_sem, recv_sem, ret_send, ret_recv, weights, load_sem) = refs[:10]
     length, seq = plan.length, plan.seq
     scale = 1.0 / math.sqrt(HEAD_DIM)
     me = lax.axis_index("seq")
 
+    loads = [
+        pltpu.make_async_copy(weight_hbm[k], weights.at[k], load_sem.at[k]) for k in range(4)
+    ]
+    for load in loads:
+        load.start()
     back[...] = jnp.zeros_like(back)
     barrier = pltpu.get_barrier_semaphore()
     for step in range(1, seq):
         pl.semaphore_signal(
             barrier, inc=1, device_id={"seq": lax.rem(me + step, seq)}, device_id_type=MESH
+        )
+    if direct:
+        pl.semaphore_signal(
+            barrier, inc=1, device_id={"dp": 1 - lax.axis_index("dp")}, device_id_type=MESH
         )
 
     perm = permutation(length)
@@ -156,10 +285,14 @@
     g = dot_nn(perm_bf, g_ref[...]).astype(BF16)
     bias_row = jnp.where(mask_ref[...] == 1, 0.0, MASKED)
     bias = jnp.sum(jnp.where(perm, jnp.broadcast_to(bias_row, perm.shape), 0.0), axis=1, keepdims=True)
-    queries = dot_nn(x, wq_ref[...]).astype(BF16)
-    keys = dot_nn(x, wk_ref[...]).astype(BF16)
-    values = dot_nn(x, wv_ref[...]).astype(BF16)
-    grads = dot_nt(g, wo_ref[...]).astype(BF16)
+    loads[0].wait()
+    queries = dot_nn(x, weights[0]).astype(BF16)
+    loads[1].wait()
+    keys = dot_nn(x, weights[1]).astype(BF16)
+    loads[2].wait()
+    values = dot_nn(x, weights[2]).astype(BF16)
+    loads[3].wait()
+    grads = dot_nt(g, weights[3]).astype(BF16)
     lane = lax.broadcasted_iota(jnp.int32, (length, PER_GROUP * LANES), 1) & (LANES - 1)
     spreads = {}
     for group in range(GROUPS):
@@ -181,7 +314,7 @@
             staged[group][head, 0] = tile0[rows, lanes]
             staged[group][head, 1] = tile1[rows, lanes]
 
-    pl.semaphore_wait(barrier, seq - 1)
+    pl.semaphore_wait(barrier, seq - 1 + (1 if direct else 0))
 
     def out_copies(group):
         size = plan.sizes[group]
@@ -271,33 +404,78 @@
     key_rows = acc[2].astype(BF16)
     value_rows = acc[3].astype(BF16)
     pairs = [(x, query_rows), (x, key_rows), (x, value_rows), (attention, g)]
+
+    def products():
+        result = dot_nn(attention, weights[3]).astype(BF16)
+        result_ref[...] = dot_tn(perm_bf, result).astype(BF16)
+        token = (
+            dot_nt(query_rows, weights[0])
+            + dot_nt(key_rows, weights[1])
+            + dot_nt(value_rows, weights[2])
+        ).astype(BF16)
+        tgrad_ref[...] = dot_tn(perm_bf, token).astype(BF16)
+
+    if not direct:
+        for which, (left, right) in enumerate(pairs):
+            product = dot_tn(left, right)
+            for target in range(seq):
+                wgrad_ref[target, which] = product[target * rows_each : (target + 1) * rows_each]
+        products()
+        return
+
+    data, core, final, core_sems, sems, final_sems, *recvs = refs[10:]
+    reducer = Reducer(rows_each, data, core, final, recvs, core_sems, sems, final_sems)
+    half = x_ref.shape[1] // 2
+
+    def second(which):
+        reducer.core_add(which)
+        for number in reducer.numbers(which):
+            reducer.start(number, 0)
+
     for which, (left, right) in enumerate(pairs):
-        product = dot_tn(left, right).astype(wgrad_ref.dtype)
+        product = dot_tn(left, right).astype(BF16)
         for target in range(seq):
-            wgrad_ref[target, which] = product[target * rows_each : (target + 1) * rows_each]
-    result = dot_nn(attention, wo_ref[...]).astype(BF16)
-    result_ref[...] = dot_tn(perm_bf, result).astype(BF16)
-    token = (
-        dot_nt(query_rows, wq_ref[...])
-        + dot_nt(key_rows, wk_ref[...])
-        + dot_nt(value_rows, wv_ref[...])
-    ).astype(BF16)
-    tgrad_ref[...] = dot_tn(perm_bf, token).astype(BF16)
-
-
-def run_layer(seq, x, mask, wq, wk, wv, wo, g, wgrad_dtype):
+            bits = tuple(target >> k & 1 for k in (3, 2, 1, 0))
+            rows = product[target * rows_each : (target + 1) * rows_each]
+            data[bits + (which, 0)] = rows[:, :half]
+            data[bits + (which, 1)] = rows[:, half:]
+        reducer.core_start(which)
+        if which > 0:
+            second(which - 1)
+    products()
+    second(3)
+    reducer.finish(wgrad_ref)
+
+
+def run_layer(seq, x, mask, wq, wk, wv, wo, g, direct):
     length, width = x.shape
     plan = Plan(seq, length)
     rows_each = width // seq
     vmem = pl.BlockSpec(memory_space=pltpu.VMEM)
+    hbm = pl.BlockSpec(memory_space=pl.ANY)
+    if direct:
+        grads_shape = (4, rows_each, width)
+        shapes = chunk_shapes(rows_each, width)
+        chunks = len(chunk_orders(rows_each))
+        extra = [
+            pltpu.VMEM((2,) * BITS + (4, 2, rows_each, width // 2), BF16),
+            pltpu.VMEM((4, 2, 2, 2, 2, rows_each, width // 2), BF16),
+            pltpu.VMEM((4, rows_each, width // 2), BF16),
+            pltpu.SemaphoreType.DMA((2, 4)),
+            pltpu.SemaphoreType.DMA((2, len(shapes))),
+            pltpu.SemaphoreType.DMA((2, chunks)),
+        ] + [pltpu.VMEM(shape, BF16) for shape in shapes]
+    else:
+        grads_shape = (seq, 4, rows_each, width)
+        extra = []
     return pl.pallas_call(
-        functools.partial(layer_kernel, plan, rows_each),
+        functools.partial(layer_kernel, plan, rows_each, direct),
         out_shape=(
             jax.ShapeDtypeStruct((length, width), BF16),
             jax.ShapeDtypeStruct((length, width), BF16),
-            jax.ShapeDtypeStruct((seq, 4, rows_each, width), wgrad_dtype),
+            jax.ShapeDtypeStruct(grads_shape, F32),
         ),
-        in_specs=[vmem] * 7,
+        in_specs=[vmem] * 2 + [hbm] * 4 + [vmem],
         out_specs=[vmem] * 3,
         scratch_shapes=[
             pltpu.VMEM((PER_GROUP, 2, plan.rows[group], LANES), BF16) for group in range(GROUPS)
@@ -311,7 +489,10 @@
             pltpu.SemaphoreType.DMA((plan.slots,)),
             pltpu.SemaphoreType.DMA((plan.slots, seq)),
             pltpu.SemaphoreType.DMA((GROUPS,)),
-        ],
+            pltpu.VMEM((4, width, width), BF16),
+            pltpu.SemaphoreType.DMA((4,)),
+        ]
+        + extra,
         compiler_params=pltpu.CompilerParams(
             collective_id=0, has_side_effects=True, vmem_limit_bytes=60 * 2**20
         ),
@@ -319,117 +500,17 @@
     )(x, mask, wq, wk, wv, wo, g)
 
 
-BITS = 4
-STREAMS = ((1, 2, 3), (2, 3, 1))
-
-
-def reduce_kernel(parts, out_ref, data, *refs):
-    recvs = refs[:-3]
-    send_sem, recv_sem, load_sem = refs[-3:]
-    me = lax.axis_index("seq")
-    dp = lax.axis_index("dp")
-    bit = [me // 2**k % 2 for k in range(BITS)]
-    barrier = pltpu.get_barrier_semaphore()
-    for k in range(BITS):
-        pl.semaphore_signal(
-            barrier, inc=1, device_id={"seq": me + 2**k - bit[k] * 2 ** (k + 1)}, device_id_type=MESH
-        )
-    pl.semaphore_signal(barrier, inc=1, device_id={"dp": 1 - dp}, device_id_type=MESH)
-    load = pltpu.make_async_copy(parts, data, load_sem)
-    load.start()
-    load.wait()
-    pl.semaphore_wait(barrier, BITS + 1)
-
-    def view(fixed, m):
-        index = [fixed.get(3 - d, slice(None)) for d in range(BITS)]
-        return tuple(index) + (m,)
-
-    def send(number, k, done, stream):
-        fixed = {b: bit[b] for b in done}
-        fixed[k] = 1 - bit[k]
-        return pltpu.make_async_remote_copy(
-            data.at[view(fixed, pl.ds(2 * stream, 2))], recvs[number], send_sem.at[number],
-            recv_sem.at[number],
-            device_id={"seq": me + 2**k - bit[k] * 2 ** (k + 1)}, device_id_type=MESH,
-        )
-
-    def add(number, k, done, stream):
-        fixed = {b: bit[b] for b in done}
-        fixed[k] = bit[k]
-        mine = view(fixed, pl.ds(2 * stream, 2))
-        data[mine] = (data[mine].astype(F32) + recvs[number][...].astype(F32)).astype(BF16)
-
-    sequences = [(0,) + s for s in STREAMS]
-    copies = []
-    for stage in range(BITS):
-        for stream in range(2):
-            number = stage * 2 + stream
-            if stage > 0:
-                before = number - 2
-                copies[before].wait_recv()
-                add(before, sequences[stream][stage - 1], sequences[stream][: stage - 1], stream)
-            copies.append(send(number, sequences[stream][stage], sequences[stream][:stage], stream))
-            copies[-1].start()
-    final = []
-    for stream in range(2):
-        before = (BITS - 1) * 2 + stream
-        number = BITS * 2 + stream
-        copies[before].wait_recv()
-        add(before, sequences[stream][BITS - 1], sequences[stream][: BITS - 1], stream)
-        mine = view(dict(enumerate(bit)), pl.ds(2 * stream, 2))
-        final.append(
-            pltpu.make_async_remote_copy(
-                data.at[mine], recvs[number], send_sem.at[number], recv_sem.at[number],
-                device_id={"dp": 1 - dp}, device_id_type=MESH,
-            )
-        )
-        final[-1].start()
-    for stream in range(2):
-        mine = view(dict(enumerate(bit)), pl.ds(2 * stream, 2))
-        final[stream].wait_recv()
-        out_ref[2 * stream : 2 * stream + 2] = (
-            data[mine].astype(F32) + recvs[BITS * 2 + stream][...].astype(F32)
-        )
-    for copy in copies + final:
-        copy.wait_send()
-
-
-def reduce_parts(parts, rows_each, width):
-    parts = parts.reshape(2, 2, 2, 2, 4, rows_each, width)
-    recvs = []
-    for stage in range(BITS):
-        recvs += [pltpu.VMEM((2,) * (BITS - 1 - stage) + (2, rows_each, width), BF16)] * 2
-    recvs += [pltpu.VMEM((2, rows_each, width), BF16)] * 2
-    return pl.pallas_call(
-        reduce_kernel,
-        out_shape=jax.ShapeDtypeStruct((4, rows_each, width), F32),
-        in_specs=[pl.BlockSpec(memory_space=pl.ANY)],
-        out_specs=pl.BlockSpec(memory_space=pltpu.VMEM),
-        scratch_shapes=[pltpu.VMEM(parts.shape, BF16)]
-        + recvs
-        + [
-            pltpu.SemaphoreType.DMA((2 * BITS + 2,)),
-            pltpu.SemaphoreType.DMA((2 * BITS + 2,)),
-            pltpu.SemaphoreType.DMA,
-        ],
-        compiler_params=pltpu.CompilerParams(
-            collective_id=1, has_side_effects=True, vmem_limit_bytes=60 * 2**20
-        ),
-        name="reduce",
-    )(parts)
-
-
 def per_device(tokens, valid_mask, w_query, w_key, w_value, w_out, result_grad):
     seq, dp = lax.axis_size("seq"), lax.axis_size("dp")
     width = tokens.shape[2]
     rows_each = width // seq
-    direct = seq == 2**BITS and dp == 2
+    direct = seq == 2**BITS and dp == 2 and rows_each % CHUNK == 0
     result, token_grads, parts = run_layer(
         seq, tokens[0], valid_mask, w_query, w_key, w_value, w_out, result_grad[0],
-        BF16 if direct else F32,
+        direct,
     )
     if direct:
-        weight_grads = reduce_parts(parts, rows_each, width)
+        weight_grads = parts
     else:
         content = parts.reshape(seq, dp, -1).transpose(1, 0, 2).reshape(-1)
         share = lax.psum_scatter(content, ("dp", "seq"), scatter_dimension=0, tiled=True)

time: 86.5 us -> 67.9 us (0.78)
  Pallas kernels: 83.3 us -> 62.6 us
  local copies, waits for them, and re-layouts: 2.32 us -> 4.41 us
    pallas_call x2 -> x1, Pallas kernels: 83.3 us -> 62.6 us  [run_layer(): pl.pallas_call(functools.partial(layer_kernel, plan, rows_each, direct),...]
    unnamed x9 -> x5, local copies, waits for them, and re-layouts: 2.32 us -> 4.41 us
where the time goes in v1:
time: 67.9 us; the launch traced here: 67.7 us
  Pallas kernels  62.6 us (92%)
  local copies, waits for them, and re-layouts  4.41 us (6%)
    pallas_call x1, Pallas kernels, run_layer(): pl.pallas_call(functools.partial(layer_kernel, plan, rows_each, direct),...  62.6 us
    unnamed x5, local copies, waits for them, and re-layouts  4.41 us

profile of v1, /device:TPU:0, one launch (start us, length us, event | category | flops | bytes accessed | tf_op | source)
XLA Modules:
  0.0 67.7 jit_solution(12446211714162373502)
XLA Ops:
  0.6 62.6 %layer.1 = (bf16[256,768]{1,0:T(8,128)(2,1)}, bf16[256,768]{1,0:T(8,128)(2,1)}, f32[4,48,768]{2,1,0:T(8,128)}) custom-call(bf16[256,768]{1,0:T(8,128)(2,1)} %bitcast.4, s32[1,256]{1,0:T(1,128)} %refs_1_.1, bf16[768,768]{1,0:T(8,128)(2,1)} %refs_2_.1, bf16[768,768]{1,0:T(8,128)(2,1)} %refs_3_.1, bf16[768,768]{1,0:T(8,128)(2,1)} %refs_4_.1, ...), custom_call_target="tpu_custom_call" | custom-call | tf_op jit(solution)/shard_map/layer/pallas_call | solution.py:471
  63.3 0.0 copy-start
  63.3 1.8 %copy.13 = bf16[1,256,768]{2,1,0:T(8,128)(2,1)} copy(bf16[1,256,768]{2,1,0:T(8,128)(2,1)} %bitcast.7) | data formatting | bytes 786432
  65.1 1.8 %copy.14 = bf16[1,256,768]{2,1,0:T(8,128)(2,1)} copy(bf16[1,256,768]{2,1,0:T(8,128)(2,1)} %bitcast.6) | data formatting | bytes 786432
  66.9 0.0 copy-done
  66.9 0.8 %copy.15 = f32[4,48,768]{2,1,0:T(8,128)} copy(f32[4,48,768]{2,1,0:T(8,128)S(1)} %copy-done) | data formatting | bytes 1179648
Async XLA Ops:
  63.3 3.6 %copy-start = (f32[4,48,768]{2,1,0:T(8,128)S(1)}, f32[4,48,768]{2,1,0:T(8,128)}, u32[]{:S(2)}) copy-start(f32[4,48,768]{2,1,0:T(8,128)} %get-tuple-element.14) | copy-start | bytes 1769476

commit v2 on v1

--- a/solution.py
+++ b/solution.py
@@ -233,12 +233,16 @@
     def numbers(self, which):
         return [n for n, chunk in enumerate(self.chunks) if chunk[0] == which]
 
+    def advance(self, which, phase):
+        if phase == 0:
+            self.core_add(which)
+        for number in self.numbers(which):
+            if phase > 0:
+                self.add(number, phase - 1)
+            self.start(number, phase)
+
     def finish(self, out_ref):
-        numbers = sorted(range(len(self.chunks)), key=lambda n: self.chunks[n][2] is FIRST_Z)
-        for stage in range(4):
-            for number in numbers:
-                self.add(number, stage)
-                self.start(number, stage + 1)
+        numbers = range(len(self.chunks))
         for number in numbers:
             self.current[number].wait_recv()
         own_at = self.view(dict(enumerate(self.bit)), slice(None), slice(None))
@@ -427,11 +431,6 @@
     reducer = Reducer(rows_each, data, core, final, recvs, core_sems, sems, final_sems)
     half = x_ref.shape[1] // 2
 
-    def second(which):
-        reducer.core_add(which)
-        for number in reducer.numbers(which):
-            reducer.start(number, 0)
-
     for which, (left, right) in enumerate(pairs):
         product = dot_tn(left, right).astype(BF16)
         for target in range(seq):
@@ -440,10 +439,13 @@
             data[bits + (which, 0)] = rows[:, :half]
             data[bits + (which, 1)] = rows[:, half:]
         reducer.core_start(which)
-        if which > 0:
-            second(which - 1)
+        if which == 2:
+            reducer.advance(0, 0)
     products()
-    second(3)
+    for step in range(1, 4 + BITS):
+        for which in range(4):
+            if 0 <= step - which <= BITS:
+                reducer.advance(which, step - which)
     reducer.finish(wgrad_ref)
 
 

time: 67.9 us -> 70.8 us (1.043)
  Pallas kernels: 62.6 us -> 65.5 us
    pallas_call x1, Pallas kernels: 62.6 us -> 65.5 us  [run_layer(): pl.pallas_call(functools.partial(layer_kernel, plan, rows_each, direct),...]
where the time goes in v2:
time: 70.8 us; the launch traced here: 70.6 us
  Pallas kernels  65.5 us (93%)
  local copies, waits for them, and re-layouts  4.41 us (6%)
    pallas_call x1, Pallas kernels, run_layer(): pl.pallas_call(functools.partial(layer_kernel, plan, rows_each, direct),...  65.5 us
    unnamed x5, local copies, waits for them, and re-layouts  4.41 us

profile of v2, /device:TPU:0, one launch (start us, length us, event | category | flops | bytes accessed | tf_op | source)
XLA Modules:
  0.0 70.6 jit_solution(14045703087943877626)
XLA Ops:
  0.6 65.5 %layer.1 = (bf16[256,768]{1,0:T(8,128)(2,1)}, bf16[256,768]{1,0:T(8,128)(2,1)}, f32[4,48,768]{2,1,0:T(8,128)}) custom-call(bf16[256,768]{1,0:T(8,128)(2,1)} %bitcast.4, s32[1,256]{1,0:T(1,128)} %refs_1_.1, bf16[768,768]{1,0:T(8,128)(2,1)} %refs_2_.1, bf16[768,768]{1,0:T(8,128)(2,1)} %refs_3_.1, bf16[768,768]{1,0:T(8,128)(2,1)} %refs_4_.1, ...), custom_call_target="tpu_custom_call" | custom-call | tf_op jit(solution)/shard_map/layer/pallas_call | solution.py:473
  66.2 0.0 copy-start
  66.2 1.8 %copy.13 = bf16[1,256,768]{2,1,0:T(8,128)(2,1)} copy(bf16[1,256,768]{2,1,0:T(8,128)(2,1)} %bitcast.7) | data formatting | bytes 786432
  68.0 1.8 %copy.14 = bf16[1,256,768]{2,1,0:T(8,128)(2,1)} copy(bf16[1,256,768]{2,1,0:T(8,128)(2,1)} %bitcast.6) | data formatting | bytes 786432
  69.8 0.0 copy-done
  69.8 0.8 %copy.15 = f32[4,48,768]{2,1,0:T(8,128)} copy(f32[4,48,768]{2,1,0:T(8,128)S(1)} %copy-done) | data formatting | bytes 1179648
Async XLA Ops:
  66.2 3.6 %copy-start = (f32[4,48,768]{2,1,0:T(8,128)S(1)}, f32[4,48,768]{2,1,0:T(8,128)}, u32[]{:S(2)}) copy-start(f32[4,48,768]{2,1,0:T(8,128)} %get-tuple-element.14) | copy-start | bytes 1769476
